TPU v7x, 32 devices: a whole 2x2x4 slice. The times are simulated.
32 devices in a mesh: row: 8 (over z, y), col: 4 (over x, core).
Axes of the slice: x: 2, y: 2, z: 4, core: 2. Of those that a mesh axis runs over, the one named last changes fastest.
Arguments:
- vectors: bfloat16 [16384, 256], P(('row', 'col'))
- tile_values: bfloat16 [8, 4, 80, 256, 256], P('row', 'col')
- tile_row: int32 [8, 4, 80], P('row', 'col'), may hold values from 0 to 7, as said below
- tile_col: int32 [8, 4, 80], P('row', 'col'), may hold values from 0 to 15, as said below
- counts: int32 [8, 4], P('row', 'col'), may hold values from 40 to 80, as said below
Outputs:
- basis: float32 [16384, 256], P(('row', 'col'))
- factor: float32 [256, 256], replicated
Inputs may be any that keep to these rules, and one draw needn't show every extreme that they name: Within one device the pairs (tile_row, tile_col) of its slots are distinct, and every tile row of a block row has a slot on every device below counts. `tile_col`: column index of a slot's tile within the device's column set. `counts`: some device fills all 80 slots in every draw.
All inputs are finite; a program needn't handle non-finite values.
Results may differ from a plain program's by a relative error of at most 0.0003.
Values may be sent and summed in bfloat16 or wider, within the bound.
A program may use at most 128 MiB of HBM per device.

v0:
```python
import jax
import jax.numpy as jnp
from jax import lax
from jax.sharding import PartitionSpec as P


def gram_of(panel, total):
    return jnp.dot(panel.T, panel, precision=lax.Precision.HIGHEST) / total


def on_device(vectors, tile_values, tile_row, tile_col, counts):
    slab = vectors.shape[0]
    width = vectors.shape[1]
    tiles_here = tile_values[0, 0]
    rows_here = tile_row[0, 0]
    cols_here = tile_col[0, 0]
    filled = counts[0, 0]
    block = tiles_here.shape[1]
    slot_count = tiles_here.shape[0]
    tile_rows = lax.axis_size("col") * slab // block
    total = slab * lax.axis_size("row") * lax.axis_size("col")
    column_set = lax.all_gather(vectors, "row", axis=0, tiled=True)
    picked = column_set.reshape(-1, block, width)[cols_here]
    prods = jnp.einsum("tij,tjk->tik", tiles_here, picked, preferred_element_type=jnp.float32)
    valid = (jnp.arange(slot_count, dtype=jnp.int32) < filled).astype(jnp.float32)
    placing = (rows_here[None, :] == jnp.arange(tile_rows, dtype=jnp.int32)[:, None]).astype(
        jnp.float32
    ) * valid[None, :]
    partial_rows = jnp.einsum("rt,tik->rik", placing, prods, precision=lax.Precision.HIGHEST)
    partial_rows = partial_rows.reshape(tile_rows * block, width)
    panel = lax.psum_scatter(partial_rows, "col", scatter_dimension=0, tiled=True)
    gram_local = gram_of(panel, total)
    lower = jnp.linalg.cholesky(lax.psum(gram_local, ("row", "col")))
    basis = jax.scipy.linalg.solve_triangular(lower, panel.T, lower=True).T
    return (basis, lower.T)


def solution(mesh):
    return jax.shard_map(
        on_device,
        mesh=mesh,
        in_specs=(
            P(("row", "col"), None),
            P("row", "col", None, None, None),
            P("row", "col", None),
            P("row", "col", None),
            P("row", "col"),
        ),
        out_specs=(P(("row", "col"), None), P()),
        check_vma=False,
    )
```

profile of v0, /device:TPU:0, one launch (start us, length us, event | category | flops | bytes accessed | tf_op | source)
XLA Modules:
  0.0 356.4 jit_solution(910897622865225886)
XLA Ops:
  7.2 0.0 all-gather.2.cloned.1.call-start
  7.2 0.7 all-gather.2.cloned.1.call-update
  7.9 0.0 reduce-scatter.2.cloned.1.call-start
  8.6 0.7 fusion.19
  9.3 52.7 %all-gather.2.cloned.1.call-done = bf16[4096,256]{1,0:T(8,128)(2,1)} async-done(((bf16[512,256]{1,0:T(8,128)(2,1)}), bf16[4096,256]{1,0:T(8,128)(2,1)}) %all-gather.2.cloned.1.call-update) | async-done | bytes 2097168 | tf_op jit(solution)/shard_map/all_gather | solution.py:22
  62.0 7.9 %gather_fusion = bf16[80,256,256]{2,1,0:T(8,128)(2,1)} fusion(bf16[16,256,256]{2,1,0:T(8,128)(2,1)} %bitcast.57, s32[1024]{0:T(1024)S(1)} %pad_clamp_fusion), kind=kCustom, calls=%fused_computation | custom fusion | bytes 20971840 | tf_op jit(solution)/shard_map/gather | solution.py:23
  69.8 13.4 %fusion.2 = f32[80,256,256]{2,1,0:T(8,128)} fusion(bf16[80,256,256]{2,1,0:T(8,128)(2,1)} %gather_fusion, bf16[1,1,80,256,256]{4,3,2,1,0:T(8,128)(2,1)} %param.6), kind=kOutput, calls=%fused_computation.5 | convolution fusion | flops 2684354560 | bytes 41943040 | tf_op jit(solution)/shard_map/tij,tjk->tik/dot_general | solution.py:24
  83.2 0.0 copy-start
  83.2 22.0 %copy.16 = f32[80,256,256]{1,0,2:T(8,128)} copy(f32[80,256,256]{2,1,0:T(8,128)} %fusion.2) | data formatting | bytes 41943040 | tf_op jit(solution)/shard_map/tij,tjk->tik/dot_general | solution.py:24
  105.2 0.0 copy-done
  105.2 12.8 %fusion = f32[8,256,256]{2,0,1:T(8,128)S(1)} fusion(f32[80,256,256]{1,0,2:T(8,128)} %copy.16, f32[80]{0:T(128)S(1)} %compare_convert_fusion, s32[80]{0:T(128)S(1)} %bitcast.61), kind=kOutput, calls=%fused_computation.3 | convolution fusion | flops 503317760 | bytes 23069312 | tf_op jit(solution)/shard_map/rt,tik->rik/dot_general | solution.py:29
  118.0 2.0 copy.11
  120.0 0.0 reduce-scatter.2.cloned.1.call-update
  120.0 0.2 all-reduce.3.cloned.1.call-start
  120.2 29.6 %reduce-scatter.2.cloned.1.call-done = f32[512,256]{1,0:T(8,128)} async-done(((f32[2048,256]{1,0:T(8,128)}), f32[512,256]{1,0:T(8,128)}) %reduce-scatter.2.cloned.1.call-update) | async-done | bytes 524304 | tf_op jit(solution)/shard_map/reduce_scatter | solution.py:31
  149.8 2.9 convolution_multiply_fusion
  152.7 0.0 all-reduce.3.cloned.1.call-update
  152.8 129.8 %all-reduce.3.cloned.1.call-done = f32[256,256]{0,1:T(8,128)} async-done(((f32[256,256]{0,1:T(8,128)}), f32[256,256]{0,1:T(8,128)}) %all-reduce.3.cloned.1.call-update) | async-done | bytes 262160 | tf_op jit(solution)/shard_map/psum | solution.py:33
  282.5 1.1 copy.13
  283.6 1.0 fusion.6
  284.6 11.7 %cholesky.50 = f32[128,128]{1,0:T(8,128)S(1)} custom-call(f32[128,128]{1,0:T(8,128)S(1)} %cholesky.118), custom_call_target="Cholesky" | custom-call | tf_op jit(solution)/shard_map/jit(cholesky)/cholesky | solution.py:33
  296.4 9.8 %custom-call.15 = f32[1,128,128]{1,2,0:T(8,128)S(1)} custom-call(f32[1,128,128]{2,1,0:T(8,128)S(1)} %get-tuple-element.29), custom_call_target="InvertDiagBlocksLowerTriangular" | custom-call | tf_op jit(solution)/shard_map/jit(cholesky)/cholesky | solution.py:33
  306.2 0.2 constant_dynamic-update-slice_fusion.1
  306.4 0.3 convolution_subtract_fusion.1
  306.7 11.7 %cholesky.105 = f32[128,128]{1,0:T(8,128)S(1)} custom-call(f32[128,128]{1,0:T(8,128)S(1)} %convolution_subtract_fusion.1), custom_call_target="Cholesky" | custom-call | tf_op jit(solution)/shard_map/jit(cholesky)/cholesky | solution.py:33
  318.5 0.7 compare_reduce_fusion
  320.6 0.1 triangular_solve.57
  320.6 4.3 %while.1 = (s32[]{:T(128)}, f32[256,256]{1,0:T(8,128)S(1)}, s32[2,2]{1,0:T(2,128)S(1)}, f32[2,128,128]{2,1,0:T(8,128)S(1)}, s32[]{:T(128)}) while((s32[]{:T(128)}, f32[256,256]{1,0:T(8,128)S(1)}, s32[2,2]{1,0:T(2,128)S(1)}, f32[2,128,128]{2,1,0:T(8,128)S(1)}, s32[]{:T(128)}) %tuple.30), condition=%wide.while_cond, body=%wide.while_body.sunk | while | flops 2 | bytes 131181 | solution.py:34
  320.8 0.6 fusion.30
  321.4 1.4 bitcast_dynamic-update-slice_fusion.2
  322.9 0.6 fusion.30
  323.5 1.4 bitcast_dynamic-update-slice_fusion.2
  324.9 19.7 %custom-call.16 = f32[2,128,128]{1,2,0:T(8,128)S(1)} custom-call(f32[2,128,128]{2,1,0:T(8,128)S(1)} %get-tuple-element.9), custom_call_target="InvertDiagBlocksLowerTriangular" | custom-call | tf_op jit(solution)/shard_map/jit(_solve_triangular)/triangular_solve | solution.py:34
  344.6 1.4 fusion.4
  346.0 1.5 convolution_subtract_fusion
  347.5 0.4 fusion.10
  348.0 1.0 copy.14
  349.0 0.8 copy.15
  (12 shorter events, 0.2 us)
Async XLA Ops:
  7.2 54.8 %all-gather.2.cloned.1.call-start = ((), (), s32[]{:S(2)}) async-start(), calls=%async_computation.1 | async-start | bytes 2359296 | tf_op jit(solution)/shard_map/all_gather | solution.py:22
  7.9 141.9 %reduce-scatter.2.cloned.1.call-start = ((), (), s32[]{:S(2)}) async-start(), calls=%async_computation.2 | async-start | bytes 2621440 | tf_op jit(solution)/shard_map/reduce_scatter | solution.py:31
  83.2 22.0 %copy-start = (s32[1,1,80]{2,1,0:T(1,128)S(1)}, s32[1,1,80]{2,1,0:T(1,128)}, u32[]{:S(2)}) copy-start(s32[1,1,80]{2,1,0:T(1,128)} %param.7) | copy-start | bytes 964
  120.0 162.6 %all-reduce.3.cloned.1.call-start = ((), (), s32[]{:S(2)}) async-start(), calls=%async_computation.3 | async-start | bytes 524288 | tf_op jit(solution)/shard_map/psum | solution.py:33
Sparse Core Ops, SparseCore 0:
  10.1 51.8 all-gather.1
  120.1 29.6 reduce-scatter.1
  155.9 126.5 all-reduce.2
where the time goes:
time: 357 us; the launch traced here: 356 us
  waiting for transfers between devices  213 us (60%)
  other arithmetic  55.4 us (16%)
  local copies, waits for them, and re-layouts  38.9 us (11%)
  matrix products  32.9 us (9%)
  between operations  15.9 us (4%)
    psum x1, waiting for transfers between devices, on_device(): lower = jnp.linalg.cholesky(lax.psum(gram_local, ('row', 'col')))  130 us
    all_gather x1, waiting for transfers between devices, on_device(): column_set = lax.all_gather(vectors, 'row', axis=0, tiled=True)  52.7 us
    another operation x6, other arithmetic, on_device(): lower = jnp.linalg.cholesky(lax.psum(gram_local, ('row', 'col')))  34 us
    reduce_scatter x1, waiting for transfers between devices, on_device(): lax.psum_scatter(partial_rows, 'col', scatter_dimension=0, tiled=True)  29.6 us
    dot_general x1, local copies, waits for them, and re-layouts, on_device(): jnp.einsum('tij,tjk->tik', tiles_here, picked, preferred_element_type=jnp...  22 us
    another operation x2, other arithmetic, on_device(): basis = jax.scipy.linalg.solve_triangular(lower, panel.T, lower=True).T  19.7 us
    dot_general x1, matrix products, on_device(): jnp.einsum('tij,tjk->tik', tiles_here, picked, preferred_element_type=jnp...  13.4 us
    dot_general x1, matrix products, on_device(): jnp.einsum('rt,tik->rik', placing, prods, precision=lax.Precision.HIGHEST)  12.8 us
  transfers between devices with their start and end apart: 3, of which 3 were waited for; matrix products, arithmetic and copies ran while one was open for 0% of the time, Pallas kernels for 0%

commit v1 on v0

v1 whole, which is shorter than its diff:
```python
import functools

import jax
import jax.numpy as jnp
from jax import lax
from jax.experimental import pallas as pl
from jax.experimental.pallas import tpu as pltpu
from jax.sharding import PartitionSpec as P

MESH = pl.DeviceIdType.MESH
HIGH = lax.Precision.HIGHEST
TILE_DMAS = 8
RS_CHUNKS = 4
CHOL_BLOCK = 32
GROUP = 8


def split_row_axis(n):
    y = 1
    while (2 * y) * (2 * y) <= n:
        y *= 2
    return n // y, y


def nearest(k, at, n):
    low = jnp.minimum(at, n - 1 - at)
    near = jnp.where(k % 2 == 1, at - (k + 1) // 2, at + k // 2)
    rest = jnp.where(at < n - 1 - at, k, n - 1 - k)
    return jnp.where(k <= 2 * low, near, rest)


def panel_kernel(
    n_row, n_col, table, vectors, tiles, panel, gram,
    vbuf, tbuf, acc, r1, r2, gpart, grecv, gfull,
    tile_sem, own_sem, ag_send, ag_recv, s1_send, s1_recv, s2_send, s2_recv,
    g_send, g_recv, f_send, f_recv,
):
    n_dev = n_row * n_col
    nz, ny = split_row_axis(n_row)
    nx = n_col // 2
    row = lax.axis_index("row")
    col = lax.axis_index("col")
    me = row * n_col + col
    z, y = row // ny, row % ny
    x, core = col // 2, col % 2
    slab, width = vectors.shape
    slots, block, _ = tiles.shape
    per_block = slab // block
    tile_rows = n_col * per_block
    tile_cols = n_row * per_block
    owners, own_rows, _ = gfull.shape

    own_copy = pltpu.make_async_copy(vectors, vbuf.at[row], own_sem)
    own_copy.start()
    per_dma = slots // TILE_DMAS
    tile_copies = [
        pltpu.make_async_copy(
            tiles.at[pl.ds(i * per_dma, per_dma)],
            tbuf.at[pl.ds(i * per_dma, per_dma)],
            tile_sem.at[i],
        )
        for i in range(TILE_DMAS)
    ]

    barrier = pltpu.get_barrier_semaphore()

    def greet(j, carry):
        peer = (me + j) % n_dev
        pl.semaphore_signal(
            barrier, inc=1, device_id=(peer // n_col, peer % n_col), device_id_type=MESH
        )
        return carry

    lax.fori_loop(1, n_dev, greet, 0)
    for copy in tile_copies:
        copy.start()
    tbuf[slots] = jnp.zeros((block, block), tbuf.dtype)
    acc[...] = jnp.zeros_like(acc)
    own_copy.wait()
    pl.semaphore_wait(barrier, n_dev - 1)

    def hop(way, b, to_row):
        return pltpu.make_async_remote_copy(
            src_ref=vbuf.at[b], dst_ref=vbuf.at[b],
            send_sem=ag_send.at[way, b], recv_sem=ag_recv.at[b],
            device_id=(to_row, col), device_id_type=MESH,
        )

    def hops(b):
        bz, by = b // ny, b % ny
        same = by == y
        return (
            (same & (bz <= z) & (z + 1 < nz), hop(0, b, jnp.minimum(row + ny, n_row - 1))),
            (same & (bz >= z) & (z >= 1), hop(1, b, jnp.maximum(row - ny, 0))),
            ((by <= y) & (y + 1 < ny), hop(2, b, jnp.minimum(row + 1, n_row - 1))),
            ((by >= y) & (y >= 1), hop(3, b, jnp.maximum(row - 1, 0))),
        )

    def gather_step(i, carry):
        b = nearest(i // ny, z, nz) * ny + nearest(i % ny, y, ny)

        @pl.when(i > 0)
        def _():
            hop(0, b, row).wait_recv()

        for needed, copy in hops(b):
            @pl.when(needed)
            def _(copy=copy):
                copy.start()

        @pl.when(i == 0)
        def _():
            for copy in tile_copies:
                copy.wait()

        for r in range(tile_rows):
            total = None
            for c in range(per_block):
                slot = table[r * tile_cols + b * per_block + c]
                part = jnp.dot(
                    tbuf[slot],
                    vbuf[b, pl.ds(c * block, block), :],
                    preferred_element_type=jnp.float32,
                )
                total = part if total is None else total + part
            rows = pl.ds(r % per_block * block, block)
            acc[r // per_block, rows, :] += total
        return carry

    lax.fori_loop(0, n_row, gather_step, 0)

    piece = slab // RS_CHUNKS

    def to_partner(xp, h):
        rows = pl.ds(h * piece, piece)
        return pltpu.make_async_remote_copy(
            src_ref=acc.at[xp * 2 + 1 - core, rows], dst_ref=r1.at[xp, rows],
            send_sem=s1_send.at[xp, h], recv_sem=s1_recv.at[xp, h],
            device_id=(row, x * 2 + 1 - core), device_id_type=MESH,
        )

    def across(xp, h):
        rows = pl.ds(h * piece, piece)
        return pltpu.make_async_remote_copy(
            src_ref=acc.at[xp * 2 + core, rows], dst_ref=r2.at[x, rows],
            send_sem=s2_send.at[xp, h], recv_sem=s2_recv.at[x, h],
            device_id=(row, xp * 2 + core), device_id_type=MESH,
        )

    def from_across(xp, h):
        rows = pl.ds(h * piece, piece)
        return pltpu.make_async_remote_copy(
            src_ref=acc.at[xp * 2 + core, rows], dst_ref=r2.at[xp, rows],
            send_sem=s2_send.at[xp, h], recv_sem=s2_recv.at[xp, h],
            device_id=(row, xp * 2 + core), device_id_type=MESH,
        )

    order = [(x + 1 + i) % nx for i in range(nx)]
    for xp in order:
        for h in range(RS_CHUNKS):
            to_partner(xp, h).start()
    for i, xp in enumerate(order):
        for h in range(RS_CHUNKS):
            rows = pl.ds(h * piece, piece)
            to_partner(xp, h).wait_recv()
            acc[xp * 2 + core, rows, :] += r1[xp, rows, :]
            if i < nx - 1:
                across(xp, h).start()
    local = None
    for h in range(RS_CHUNKS):
        rows = pl.ds(h * piece, piece)
        value = acc[x * 2 + core, rows, :]
        for xp in order[:-1]:
            from_across(xp, h).wait_recv()
            value = value + r2[xp, rows, :]
        panel[rows, :] = value
        part = lax.dot_general(
            value, value, (((0,), (0,)), ((), ())),
            precision=HIGH, preferred_element_type=jnp.float32,
        )
        local = part if local is None else local + part
    gpart[...] = (local / (slab * n_dev)).reshape(owners, own_rows, width)

    def to_owner(o):
        return pltpu.make_async_remote_copy(
            src_ref=gpart.at[o], dst_ref=grecv.at[me],
            send_sem=g_send.at[o], recv_sem=g_recv.at[me],
            device_id=(o // n_col, o % n_col), device_id_type=MESH,
        )

    def from_member(s):
        return pltpu.make_async_remote_copy(
            src_ref=gpart.at[0], dst_ref=grecv.at[s],
            send_sem=g_send.at[0], recv_sem=g_recv.at[s],
            device_id=(s // n_col, s % n_col), device_id_type=MESH,
        )

    def spread(o, s):
        return pltpu.make_async_remote_copy(
            src_ref=gfull.at[o], dst_ref=gfull.at[o],
            send_sem=f_send.at[s], recv_sem=f_recv.at[o],
            device_id=(s // n_col, s % n_col), device_id_type=MESH,
        )

    def each_peer(fn):
        def step(j, carry):
            fn((me + j) % n_dev)
            return carry
        lax.fori_loop(1, n_dev, step, 0)

    def each_owner(fn):
        def checked(o):
            if owners == n_dev:
                fn(o)
            else:
                @pl.when(o < owners)
                def _():
                    fn(o)
        each_peer(checked)

    def if_owner(fn):
        if owners == n_dev:
            fn()
        else:
            pl.when(me < owners)(fn)

    each_owner(lambda o: to_owner(o).start())

    def reduce_mine():
        grecv[me] = gpart[me]
        each_peer(lambda s: from_member(s).wait_recv())
        gfull[me] = jnp.sum(grecv[...], axis=0)
        each_peer(lambda s: spread(me, s).start())

    if_owner(reduce_mine)
    each_owner(lambda o: spread(o, me).wait_recv())
    gram[...] = gfull[...].reshape(width, width)

    each_owner(lambda o: to_owner(o).wait_send())
    if_owner(lambda: each_peer(lambda s: spread(me, s).wait_send()))
    for xp in order:
        for h in range(RS_CHUNKS):
            to_partner(xp, h).wait_send()
    for xp in order[:-1]:
        for h in range(RS_CHUNKS):
            across(xp, h).wait_send()

    def drain(b, carry):
        for needed, copy in hops(b):
            @pl.when(needed)
            def _(copy=copy):
                copy.wait_send()
        return carry

    lax.fori_loop(0, n_row, drain, 0)


def invert_factor(diag):
    n = diag.shape[0]
    lanes = 128
    rows = lax.broadcasted_iota(jnp.int32, (n, lanes), 0)
    cols = lax.broadcasted_iota(jnp.int32, (n, lanes), 1)
    eye = (cols - n == rows).astype(jnp.float32)
    work = jnp.concatenate([diag, eye[:, n:]], axis=1)
    scale = jnp.zeros((n, lanes), jnp.float32)
    for start in range(0, n, GROUP):
        picked = [
            jnp.broadcast_to(work[:, start + j : start + j + 1], (n, lanes))
            for j in range(GROUP)
        ]
        for j in range(GROUP):
            at = start + j
            pivot = picked[j][at : at + 1, :]
            scale = jnp.where(rows == at, lax.rsqrt(pivot), scale)
            weight = jnp.where(rows > at, picked[j] * (1.0 / pivot), 0.0)
            for later in range(j + 1, GROUP):
                picked[later] = picked[later] - weight * picked[later][at : at + 1, :]
            work = work - weight * work[at : at + 1, :]
    return (work * scale)[:, n : 2 * n]


def factor_kernel(gram, panel, basis, upper, work):
    width = gram.shape[0]
    n = CHOL_BLOCK
    rows = lax.broadcasted_iota(jnp.int32, (width, width), 0)
    cols = lax.broadcasted_iota(jnp.int32, (width, width), 1)
    work[:, :width] = gram[...]
    work[:, width:] = (rows == cols).astype(jnp.float32)
    for start in range(0, width, n):
        stop = start + n
        inverse = invert_factor(work[start:stop, start:stop])
        done = jnp.dot(
            inverse, work[start:stop, :], precision=HIGH, preferred_element_type=jnp.float32
        )
        work[start:stop, :] = done
        if stop < width:
            work[stop:, :] -= lax.dot_general(
                done[:, stop:width], done, (((0,), (0,)), ((), ())),
                precision=HIGH, preferred_element_type=jnp.float32,
            )
    upper[...] = jnp.where(cols >= rows, work[:, :width], 0.0)
    basis[...] = lax.dot_general(
        panel[...], work[:, width:], (((1,), (1,)), ((), ())),
        precision=HIGH, preferred_element_type=jnp.float32,
    )


def on_device(n_row, n_col, vectors, tile_values, tile_row, tile_col, counts):
    slab, width = vectors.shape
    tiles = tile_values[0, 0]
    slots, block, _ = tiles.shape
    n_dev = n_row * n_col
    per_block = slab // block
    tile_rows, tile_cols = n_col * per_block, n_row * per_block
    number = jnp.arange(slots, dtype=jnp.int32)
    place = tile_row[0, 0] * tile_cols + tile_col[0, 0]
    place = jnp.where(number < counts[0, 0], place, -1)
    cell = jnp.arange(tile_rows * tile_cols, dtype=jnp.int32)
    table = jnp.min(jnp.where(cell[:, None] == place[None, :], number[None, :], slots), axis=1)
    own_rows = max(8, width // n_dev)
    owners = width // own_rows
    nx = n_col // 2
    vmem = pl.BlockSpec(memory_space=pltpu.VMEM)
    f32 = jnp.float32
    panel, gram = pl.pallas_call(
        functools.partial(panel_kernel, n_row, n_col),
        out_shape=(
            jax.ShapeDtypeStruct((slab, width), f32),
            jax.ShapeDtypeStruct((width, width), f32),
        ),
        in_specs=[
            pl.BlockSpec(memory_space=pltpu.SMEM),
            pl.BlockSpec(memory_space=pl.ANY),
            pl.BlockSpec(memory_space=pl.ANY),
        ],
        out_specs=(vmem, vmem),
        scratch_shapes=[
            pltpu.VMEM((n_row, slab, width), vectors.dtype),
            pltpu.VMEM((slots + 1, block, block), tiles.dtype),
            pltpu.VMEM((n_col, slab, width), f32),
            pltpu.VMEM((nx, slab, width), f32),
            pltpu.VMEM((nx, slab, width), f32),
            pltpu.VMEM((owners, own_rows, width), f32),
            pltpu.VMEM((n_dev, own_rows, width), f32),
            pltpu.VMEM((owners, own_rows, width), f32),
            pltpu.SemaphoreType.DMA((TILE_DMAS,)),
            pltpu.SemaphoreType.DMA,
            pltpu.SemaphoreType.DMA((4, n_row)),
            pltpu.SemaphoreType.DMA((n_row,)),
            pltpu.SemaphoreType.DMA((nx, RS_CHUNKS)),
            pltpu.SemaphoreType.DMA((nx, RS_CHUNKS)),
            pltpu.SemaphoreType.DMA((nx, RS_CHUNKS)),
            pltpu.SemaphoreType.DMA((nx, RS_CHUNKS)),
            pltpu.SemaphoreType.DMA((owners,)),
            pltpu.SemaphoreType.DMA((n_dev,)),
            pltpu.SemaphoreType.DMA((n_dev,)),
            pltpu.SemaphoreType.DMA((owners,)),
        ],
        compiler_params=pltpu.CompilerParams(
            collective_id=0, has_side_effects=True, vmem_limit_bytes=56 << 20
        ),
        name="panel",
    )(table, vectors, tiles)
    basis, upper = pl.pallas_call(
        factor_kernel,
        out_shape=(
            jax.ShapeDtypeStruct((slab, width), f32),
            jax.ShapeDtypeStruct((width, width), f32),
        ),
        in_specs=[vmem, vmem],
        out_specs=(vmem, vmem),
        scratch_shapes=[pltpu.VMEM((width, 2 * width), f32)],
        name="factor",
    )(gram, panel)
    return (basis, upper)


def solution(mesh):
    n_row, n_col = mesh.shape["row"], mesh.shape["col"]
    return jax.shard_map(
        functools.partial(on_device, n_row, n_col),
        mesh=mesh,
        in_specs=(
            P(("row", "col"), None),
            P("row", "col", None, None, None),
            P("row", "col", None),
            P("row", "col", None),
            P("row", "col"),
        ),
        out_specs=(P(("row", "col"), None), P()),
        check_vma=False,
    )
```

time: 357 us -> 92.1 us (0.26)
  waiting for transfers between devices: 213 us -> 0 us
  Pallas kernels: 0 us -> 89 us
  other arithmetic: 55.4 us -> 1.28 us
  local copies, waits for them, and re-layouts: 38.9 us -> 0 us
  matrix products: 32.9 us -> 0 us
  between operations: 15.9 us -> 1.29 us
    psum x1 -> x0, waiting for transfers between devices: 130 us -> none  [on_device(): lower = jnp.linalg.cholesky(lax.psum(gram_local, ('row', 'col')))]
    pallas_call x0 -> x2, Pallas kernels: none -> 89 us  [the longest x1 74.9 us: on_device(): pl.pallas_call(functools.partial(panel_kernel, n_row, n_col), out_shape=(...]
    another operation x8 -> x0, other arithmetic: 53.7 us -> none  [the longest x6 34 us: on_device(): lower = jnp.linalg.cholesky(lax.psum(gram_local, ('row', 'col')))]
    all_gather x1 -> x0, waiting for transfers between devices: 52.7 us -> none  [on_device(): column_set = lax.all_gather(vectors, 'row', axis=0, tiled=True)]
    reduce_scatter x1 -> x0, waiting for transfers between devices: 29.6 us -> none  [on_device(): lax.psum_scatter(partial_rows, 'col', scatter_dimension=0, tiled=True)]
    dot_general x3 -> x0, matrix products: 29.1 us -> none  [the longest x1 13.4 us: on_device(): jnp.einsum('tij,tjk->tik', tiles_here, picked, preferred_element_type=jnp...]
    dot_general x2 -> x0, local copies, waits for them, and re-layouts: 23.9 us -> none  [the longest x1 22 us: on_device(): jnp.einsum('tij,tjk->tik', tiles_here, picked, preferred_element_type=jnp...]
    gather x1 -> x0, local copies, waits for them, and re-layouts: 7.87 us -> none  [on_device(): picked = column_set.reshape(-1, block, width)[cols_here]]
  transfers between devices with their start and end apart: 3 -> 0, of which waited for: 3 -> 0; matrix products, arithmetic and copies ran while one was open for 0% -> 0% of each run, Pallas kernels for 0% -> 0%
where the time goes in v1:
time: 92.1 us; the launch traced here: 91.5 us
  Pallas kernels  89 us (97%)
  between operations  1.29 us (1%)
  other arithmetic  1.28 us (1%)
    pallas_call x1, Pallas kernels, on_device(): pl.pallas_call(functools.partial(panel_kernel, n_row, n_col), out_shape=(...  74.9 us
    pallas_call x1, Pallas kernels, on_device(): pl.pallas_call(factor_kernel, out_shape=(jax.ShapeDtypeStruct((slab, widt...  14.1 us

profile of v1, /device:TPU:0, one launch (start us, length us, event | category | flops | bytes accessed | tf_op | source)
XLA Modules:
  0.0 91.5 jit_solution(1198473384374856984)
XLA Ops:
  1.3 0.7 compare_select_fusion
  2.0 0.6 select_reduce_fusion.table
  2.6 74.9 %panel.1 = (f32[512,256]{1,0:T(8,128)}, f32[256,256]{1,0:T(8,128)}) custom-call(s32[128]{0:T(128)} %select_reduce_fusion.table, bf16[512,256]{1,0:T(8,128)(2,1)} %vectors.1, bf16[80,256,256]{2,1,0:T(8,128)(2,1)} %bitcast.5), custom_call_target="tpu_custom_call" | custom-call | tf_op jit(solution)/shard_map/panel/pallas_call | solution.py:325
  77.5 14.1 %factor.1 = (f32[512,256]{1,0:T(8,128)}, f32[256,256]{1,0:T(8,128)}) custom-call(f32[256,256]{1,0:T(8,128)} %get-tuple-element.4.gram, f32[512,256]{1,0:T(8,128)} %get-tuple-element.5.panel), custom_call_target="tpu_custom_call" | custom-call | tf_op jit(solution)/shard_map/factor/pallas_call | solution.py:364

commit v2 on v1

v2 whole, which is shorter than its diff:
```python
import functools

import jax
import jax.numpy as jnp
from jax import lax
from jax.experimental import pallas as pl
from jax.experimental.pallas import tpu as pltpu
from jax.sharding import PartitionSpec as P

MESH = pl.DeviceIdType.MESH
HIGH = lax.Precision.HIGHEST
TILE_DMAS = 8
RS_CHUNKS = 4
CHOL_BLOCK = 64
GROUP = 16


def split_row_axis(n):
    y = 1
    while (2 * y) * (2 * y) <= n:
        y *= 2
    return n // y, y


def nearest(k, at, n):
    low = jnp.minimum(at, n - 1 - at)
    near = jnp.where(k % 2 == 1, at - (k + 1) // 2, at + k // 2)
    rest = jnp.where(at < n - 1 - at, k, n - 1 - k)
    return jnp.where(k <= 2 * low, near, rest)


def visit(i, z, y, nz, ny):
    if ny == 2 and nz > 1:
        last = i == nz * ny - 1
        along = (i % 2 == 1) & ~last
        k = jnp.where(along, (i + 1) // 2, i // 2 - 1)
        k = jnp.where(i == 0, 0, jnp.where(last, nz - 1, k))
        j = jnp.where(along | (i == 0), 0, 1)
    else:
        k, j = i // ny, i % ny
    return nearest(k, z, nz) * ny + nearest(j, y, ny)


def panel_kernel(
    n_row, n_col, table, vectors, tiles, panel, gram,
    vbuf, tbuf, acc, r1, r2, gpart, grecv, gfull,
    tile_sem, own_sem, ag_send, ag_recv, s1_send, s1_recv, s2_send, s2_recv,
    g_send, g_recv, f_send, f_recv,
):
    n_dev = n_row * n_col
    nz, ny = split_row_axis(n_row)
    nx = n_col // 2
    row = lax.axis_index("row")
    col = lax.axis_index("col")
    me = row * n_col + col
    z, y = row // ny, row % ny
    x, core = col // 2, col % 2
    slab, width = vectors.shape
    slots, block, _ = tiles.shape
    half = width // 2
    per_block = slab // block
    tile_rows = n_col * per_block
    tile_cols = n_row * per_block
    pieces = gfull.shape[0]
    passes = grecv.shape[0]

    own_copies = [
        pltpu.make_async_copy(
            vectors.at[:, pl.ds(k * half, half)], vbuf.at[k, row], own_sem.at[k]
        )
        for k in range(2)
    ]
    for copy in own_copies:
        copy.start()
    per_dma = slots // TILE_DMAS
    tile_copies = [
        pltpu.make_async_copy(
            tiles.at[pl.ds(i * per_dma, per_dma)],
            tbuf.at[pl.ds(i * per_dma, per_dma)],
            tile_sem.at[i],
        )
        for i in range(TILE_DMAS)
    ]

    barrier = pltpu.get_barrier_semaphore()

    def greet(j, carry):
        peer = (me + j) % n_dev
        pl.semaphore_signal(
            barrier, inc=1, device_id=(peer // n_col, peer % n_col), device_id_type=MESH
        )
        return carry

    lax.fori_loop(1, n_dev, greet, 0)
    for copy in tile_copies:
        copy.start()
    tbuf[slots] = jnp.zeros((block, block), tbuf.dtype)
    acc[...] = jnp.zeros_like(acc)
    for copy in own_copies:
        copy.wait()
    pl.semaphore_wait(barrier, n_dev - 1)

    def hop(way, k, b, to_row):
        return pltpu.make_async_remote_copy(
            src_ref=vbuf.at[k, b], dst_ref=vbuf.at[k, b],
            send_sem=ag_send.at[way, k, b], recv_sem=ag_recv.at[k, b],
            device_id=(to_row, col), device_id_type=MESH,
        )

    def hops(k, b):
        bz, by = b // ny, b % ny
        same = by == y
        return (
            (same & (bz <= z) & (z + 1 < nz), hop(0, k, b, jnp.minimum(row + ny, n_row - 1))),
            (same & (bz >= z) & (z >= 1), hop(1, k, b, jnp.maximum(row - ny, 0))),
            ((by <= y) & (y + 1 < ny), hop(2, k, b, jnp.minimum(row + 1, n_row - 1))),
            ((by >= y) & (y >= 1), hop(3, k, b, jnp.maximum(row - 1, 0))),
        )

    def pass_on(k, b):
        for needed, copy in hops(k, b):
            @pl.when(needed)
            def _(copy=copy):
                copy.start()

    piece = slab // RS_CHUNKS
    order = [(x + 1 + i) % nx for i in range(nx)]

    def to_partner(k, xp, h):
        rows = pl.ds(h * piece, piece)
        return pltpu.make_async_remote_copy(
            src_ref=acc.at[k, xp * 2 + 1 - core, rows], dst_ref=r1.at[k, xp, rows],
            send_sem=s1_send.at[k, xp, h], recv_sem=s1_recv.at[k, xp, h],
            device_id=(row, x * 2 + 1 - core), device_id_type=MESH,
        )

    def across(k, xp, h, slot):
        rows = pl.ds(h * piece, piece)
        return pltpu.make_async_remote_copy(
            src_ref=acc.at[k, xp * 2 + core, rows], dst_ref=r2.at[k, slot, rows],
            send_sem=s2_send.at[k, xp, h], recv_sem=s2_recv.at[k, slot, h],
            device_id=(row, xp * 2 + core), device_id_type=MESH,
        )

    def give(k):
        for xp in order:
            for h in range(RS_CHUNKS):
                to_partner(k, xp, h).start()

    def take(k):
        for i, xp in enumerate(order):
            for h in range(RS_CHUNKS):
                rows = pl.ds(h * piece, piece)
                to_partner(k, xp, h).wait_recv()
                acc[k, xp * 2 + core, rows, :] += r1[k, xp, rows, :]
                if i < nx - 1:
                    across(k, xp, h, x).start()

    def finish(k, h):
        rows = pl.ds(h * piece, piece)
        value = acc[k, x * 2 + core, rows, :]
        for xp in order[:-1]:
            across(k, xp, h, xp).wait_recv()
            value = value + r2[k, xp, rows, :]
        panel[rows, k * half : (k + 1) * half] = value
        return value

    pass_on(0, row)

    def gather_step(i, carry):
        k, s = i // n_row, i % n_row
        b = visit(s, z, y, nz, ny)

        @pl.when(s > 0)
        def _():
            hop(0, k, b, row).wait_recv()
            pass_on(k, b)

        @pl.when(i == n_row // 2)
        def _():
            pass_on(1, row)

        @pl.when(i == 0)
        def _():
            for copy in tile_copies:
                copy.wait()

        for r in range(tile_rows):
            total = None
            for c in range(per_block):
                slot = table[r * tile_cols + b * per_block + c]
                part = jnp.dot(
                    tbuf[slot],
                    vbuf[k, b, pl.ds(c * block, block), :],
                    preferred_element_type=jnp.float32,
                )
                total = part if total is None else total + part
            rows = pl.ds(r % per_block * block, block)
            acc[k, r // per_block, rows, :] += total

        @pl.when(i == n_row - 1)
        def _():
            give(0)

        @pl.when(i == n_row + 1)
        def _():
            take(0)

        return carry

    lax.fori_loop(0, 2 * n_row, gather_step, 0)

    give(1)
    take(1)

    def gram_part(a, b):
        return lax.dot_general(
            a, b, (((0,), (0,)), ((), ())),
            precision=HIGH, preferred_element_type=jnp.float32,
        )

    g00 = g01 = g11 = jnp.zeros((half, half), jnp.float32)
    for h in range(RS_CHUNKS):
        value = finish(0, h)
        g00 = g00 + gram_part(value, value)
    for h in range(RS_CHUNKS):
        value = finish(1, h)
        g01 = g01 + gram_part(panel[pl.ds(h * piece, piece), :half], value)
        g11 = g11 + gram_part(value, value)

    total_rows = slab * n_dev
    rows = lax.broadcasted_iota(jnp.int32, (half, half), 0)
    cols = lax.broadcasted_iota(jnp.int32, (half, half), 1)
    each = half // 8
    gpart[0:each] = (g01 / total_rows).reshape(each, 8, half)
    gpart[each : 2 * each] = (jnp.where(rows > cols, g00, g11) / total_rows).reshape(each, 8, half)
    diagonal = jnp.sum(jnp.where(rows == cols, g00, 0.0), axis=0, keepdims=True)
    gpart[2 * each] = jnp.broadcast_to(diagonal / total_rows, (8, half))

    def to_owner(p, o):
        t = p * n_dev + o
        return pltpu.make_async_remote_copy(
            src_ref=gpart.at[t], dst_ref=grecv.at[p, me],
            send_sem=g_send.at[t], recv_sem=g_recv.at[p, me],
            device_id=(o // n_col, o % n_col), device_id_type=MESH,
        )

    def from_member(p, s):
        return pltpu.make_async_remote_copy(
            src_ref=gpart.at[0], dst_ref=grecv.at[p, s],
            send_sem=g_send.at[0], recv_sem=g_recv.at[p, s],
            device_id=(s // n_col, s % n_col), device_id_type=MESH,
        )

    def spread(p, o, s):
        t = p * n_dev + o
        return pltpu.make_async_remote_copy(
            src_ref=gfull.at[t], dst_ref=gfull.at[t],
            send_sem=f_send.at[p, s], recv_sem=f_recv.at[t],
            device_id=(s // n_col, s % n_col), device_id_type=MESH,
        )

    def each_peer(fn):
        def step(j, carry):
            fn((me + j) % n_dev)
            return carry
        lax.fori_loop(1, n_dev, step, 0)

    def owned(p, o, fn):
        if (p + 1) * n_dev <= pieces:
            fn()
        else:
            pl.when(p * n_dev + o < pieces)(fn)

    def each_owner(p, fn):
        each_peer(lambda o: owned(p, o, lambda: fn(o)))

    for p in range(passes):
        each_owner(p, lambda o, p=p: to_owner(p, o).start())

    for p in range(passes):
        def reduce_mine(p=p):
            t = p * n_dev + me
            grecv[p, me] = gpart[t]
            each_peer(lambda s: from_member(p, s).wait_recv())
            gfull[t] = jnp.sum(grecv[p], axis=0)
            each_peer(lambda s: spread(p, me, s).start())

        owned(p, me, reduce_mine)
    for p in range(passes):
        each_owner(p, lambda o, p=p: spread(p, o, me).wait_recv())

    mixed = gfull[each : 2 * each].reshape(half, half)
    below = jnp.where(rows > cols, mixed, 0.0)
    above = jnp.where(rows < cols, mixed, 0.0)
    gram[:half, :half] = jnp.where(
        rows == cols, jnp.broadcast_to(gfull[2 * each, 0:1, :], (half, half)), below + below.T
    )
    gram[:half, half:] = gfull[0:each].reshape(half, half)
    gram[half:, :half] = jnp.zeros((half, half), jnp.float32)
    gram[half:, half:] = jnp.where(rows == cols, mixed, above + above.T)

    for p in range(passes):
        each_owner(p, lambda o, p=p: to_owner(p, o).wait_send())
        owned(p, me, lambda p=p: each_peer(lambda s: spread(p, me, s).wait_send()))
    for k in range(2):
        for xp in order:
            for h in range(RS_CHUNKS):
                to_partner(k, xp, h).wait_send()
        for xp in order[:-1]:
            for h in range(RS_CHUNKS):
                across(k, xp, h, x).wait_send()

    def drain(i, carry):
        for needed, copy in hops(i // n_row, i % n_row):
            @pl.when(needed)
            def _(copy=copy):
                copy.wait_send()
        return carry

    lax.fori_loop(0, 2 * n_row, drain, 0)


def invert_factor(diag):
    n = diag.shape[0]
    lanes = 128
    rows = lax.broadcasted_iota(jnp.int32, (n, lanes), 0)
    cols = lax.broadcasted_iota(jnp.int32, (n, lanes), 1)
    eye = (cols - n == rows).astype(jnp.float32)
    work = jnp.concatenate([diag, eye[:, n:]], axis=1)
    scale = jnp.zeros((n, lanes), jnp.float32)
    for start in range(0, n, GROUP):
        picked = [
            jnp.broadcast_to(work[:, start + j : start + j + 1], (n, lanes))
            for j in range(GROUP)
        ]
        for j in range(GROUP):
            at = start + j
            pivot = picked[j][at : at + 1, :]
            root = lax.rsqrt(pivot)
            scale = jnp.where(rows == at, root, scale)
            weight = jnp.where(rows > at, picked[j] * (root * root), 0.0)
            for later in range(j + 1, GROUP):
                picked[later] = picked[later] - weight * picked[later][at : at + 1, :]
            work = work - weight * work[at : at + 1, :]
    return (work * scale)[:, n : 2 * n]


def factor_kernel(gram, panel, basis, upper, work):
    width = gram.shape[0]
    n = CHOL_BLOCK
    rows = lax.broadcasted_iota(jnp.int32, (width, width), 0)
    cols = lax.broadcasted_iota(jnp.int32, (width, width), 1)
    work[:, :width] = gram[...]
    work[:, width:] = (rows == cols).astype(jnp.float32)
    for start in range(0, width, n):
        stop = start + n
        inverse = invert_factor(work[start:stop, start:stop])
        done = jnp.dot(
            inverse, work[start:stop, :], precision=HIGH, preferred_element_type=jnp.float32
        )
        work[start:stop, :] = done
        if stop < width:
            work[stop:, :] -= lax.dot_general(
                done[:, stop:width], done, (((0,), (0,)), ((), ())),
                precision=HIGH, preferred_element_type=jnp.float32,
            )
    upper[...] = jnp.where(cols >= rows, work[:, :width], 0.0)
    basis[...] = lax.dot_general(
        panel[...], work[:, width:], (((1,), (1,)), ((), ())),
        precision=HIGH, preferred_element_type=jnp.float32,
    )


def on_device(n_row, n_col, vectors, tile_values, tile_row, tile_col, counts):
    slab, width = vectors.shape
    tiles = tile_values[0, 0]
    slots, block, _ = tiles.shape
    n_dev = n_row * n_col
    per_block = slab // block
    tile_rows, tile_cols = n_col * per_block, n_row * per_block
    number = jnp.arange(slots, dtype=jnp.int32)
    place = tile_row[0, 0] * tile_cols + tile_col[0, 0]
    place = jnp.where(number < counts[0, 0], place, -1)
    cell = jnp.arange(tile_rows * tile_cols, dtype=jnp.int32)
    table = jnp.min(jnp.where(cell[:, None] == place[None, :], number[None, :], slots), axis=1)
    half = width // 2
    pieces = 2 * (half // 8) + 1
    passes = pl.cdiv(pieces, n_dev)
    nx = n_col // 2
    vmem = pl.BlockSpec(memory_space=pltpu.VMEM)
    f32 = jnp.float32
    panel, gram = pl.pallas_call(
        functools.partial(panel_kernel, n_row, n_col),
        out_shape=(
            jax.ShapeDtypeStruct((slab, width), f32),
            jax.ShapeDtypeStruct((width, width), f32),
        ),
        in_specs=[
            pl.BlockSpec(memory_space=pltpu.SMEM),
            pl.BlockSpec(memory_space=pl.ANY),
            pl.BlockSpec(memory_space=pl.ANY),
        ],
        out_specs=(vmem, vmem),
        scratch_shapes=[
            pltpu.VMEM((2, n_row, slab, half), vectors.dtype),
            pltpu.VMEM((slots + 1, block, block), tiles.dtype),
            pltpu.VMEM((2, n_col, slab, half), f32),
            pltpu.VMEM((2, nx, slab, half), f32),
            pltpu.VMEM((2, nx, slab, half), f32),
            pltpu.VMEM((pieces, 8, half), f32),
            pltpu.VMEM((passes, n_dev, 8, half), f32),
            pltpu.VMEM((pieces, 8, half), f32),
            pltpu.SemaphoreType.DMA((TILE_DMAS,)),
            pltpu.SemaphoreType.DMA((2,)),
            pltpu.SemaphoreType.DMA((4, 2, n_row)),
            pltpu.SemaphoreType.DMA((2, n_row)),
            pltpu.SemaphoreType.DMA((2, nx, RS_CHUNKS)),
            pltpu.SemaphoreType.DMA((2, nx, RS_CHUNKS)),
            pltpu.SemaphoreType.DMA((2, nx, RS_CHUNKS)),
            pltpu.SemaphoreType.DMA((2, nx, RS_CHUNKS)),
            pltpu.SemaphoreType.DMA((pieces,)),
            pltpu.SemaphoreType.DMA((passes, n_dev)),
            pltpu.SemaphoreType.DMA((passes, n_dev)),
            pltpu.SemaphoreType.DMA((pieces,)),
        ],
        compiler_params=pltpu.CompilerParams(
            collective_id=0, has_side_effects=True, vmem_limit_bytes=56 << 20
        ),
        name="panel",
    )(table, vectors, tiles)
    basis, upper = pl.pallas_call(
        factor_kernel,
        out_shape=(
            jax.ShapeDtypeStruct((slab, width), f32),
            jax.ShapeDtypeStruct((width, width), f32),
        ),
        in_specs=[vmem, vmem],
        out_specs=(vmem, vmem),
        scratch_shapes=[pltpu.VMEM((width, 2 * width), f32)],
        name="factor",
    )(gram, panel)
    return (basis, upper)


def solution(mesh):
    n_row, n_col = mesh.shape["row"], mesh.shape["col"]
    return jax.shard_map(
        functools.partial(on_device, n_row, n_col),
        mesh=mesh,
        in_specs=(
            P(("row", "col"), None),
            P("row", "col", None, None, None),
            P("row", "col", None),
            P("row", "col", None),
            P("row", "col"),
        ),
        out_specs=(P(("row", "col"), None), P()),
        check_vma=False,
    )
```

time: 92.1 us -> 82.2 us (0.89)
  Pallas kernels: 89 us -> 79.4 us
    pallas_call x1, Pallas kernels: 74.9 us -> 68 us  [on_device(): pl.pallas_call(functools.partial(panel_kernel, n_row, n_col), out_shape=(...]
    pallas_call x1, Pallas kernels: 14.1 us -> 11.5 us  [on_device(): pl.pallas_call(factor_kernel, out_shape=(jax.ShapeDtypeStruct((slab, widt...]
where the time goes in v2:
time: 82.2 us; the launch traced here: 82 us
  Pallas kernels  79.4 us (97%)
  between operations  1.29 us (2%)
  other arithmetic  1.28 us (2%)
    pallas_call x1, Pallas kernels, on_device(): pl.pallas_call(functools.partial(panel_kernel, n_row, n_col), out_shape=(...  68 us
    pallas_call x1, Pallas kernels, on_device(): pl.pallas_call(factor_kernel, out_shape=(jax.ShapeDtypeStruct((slab, widt...  11.5 us

profile of v2, /device:TPU:0, one launch (start us, length us, event | category | flops | bytes accessed | tf_op | source)
XLA Modules:
  0.0 82.0 jit_solution(4277559249979373448)
XLA Ops:
  1.3 0.7 compare_select_fusion
  2.0 0.6 select_reduce_fusion.table
  2.6 68.0 %panel.1 = (f32[512,256]{1,0:T(8,128)}, f32[256,256]{1,0:T(8,128)}) custom-call(s32[128]{0:T(128)} %select_reduce_fusion.table, bf16[512,256]{1,0:T(8,128)(2,1)} %vectors.1, bf16[80,256,256]{2,1,0:T(8,128)(2,1)} %bitcast.5), custom_call_target="tpu_custom_call" | custom-call | tf_op jit(solution)/shard_map/panel/pallas_call | solution.py:393
  70.5 11.5 %factor.1 = (f32[512,256]{1,0:T(8,128)}, f32[256,256]{1,0:T(8,128)}) custom-call(f32[256,256]{1,0:T(8,128)} %get-tuple-element.4.gram, f32[512,256]{1,0:T(8,128)} %get-tuple-element.5.panel), custom_call_target="tpu_custom_call" | custom-call | tf_op jit(solution)/shard_map/factor/pallas_call | solution.py:432
